TPU v7x, 32 devices: a whole 2x2x4 slice. The times are simulated.
32 devices in a mesh: row: 4 (over y, x), col: 8 (over z, core).
Axes of the slice: x: 2, y: 2, z: 4, core: 2. Of those that a mesh axis runs over, the one named last changes fastest.
Arguments:
- feat_rows: float32 [2048, 512], P(('row', 'col')), may hold values from -0.6 to 0.6
- feat_cols: float32 [2048, 512], P(('col', 'row')), may hold values from -0.6 to 0.6
- panel_rows: float32 [2048, 1024], P(('row', 'col')), may hold values from -0.6 to 0.6
- panel_cols: float32 [2048, 1024], P(('col', 'row')), may hold values from -0.6 to 0.6
- accumulator: float32 [2048, 2048], P('row', 'col'), may hold values from -1.8 to 1.8
Outputs:
- acc_new: float32 [2048, 2048], P('row', 'col')
- grad_rows: float32 [2048, 512], P(('row', 'col'))
- grad_cols: float32 [2048, 512], P(('col', 'row'))
All inputs are finite; a program needn't handle non-finite values.
Results may differ from a plain program's by a relative error of at most 0.00011.
Values sent between devices are 32-bit elements; how exact they have to be, the bound alone decides.
A program may use at most 64 MiB of HBM per device.

v0:
```python
import jax
import jax.numpy as jnp
from jax import lax
from jax.sharding import PartitionSpec as P

decay_rate = 0.125
grad_scale = 0.25


def local_tile(rows_feat, rows_panel, acc_tile, cols_feat, cols_panel):
    grams_tile = acc_tile + jnp.dot(rows_panel, cols_panel.T, precision=lax.Precision.HIGHEST)
    cross_term = jnp.dot(rows_feat, cols_feat.T, precision=lax.Precision.HIGHEST)
    norm_rows = jnp.sum(rows_feat * rows_feat, axis=1)
    norm_cols = jnp.sum(cols_feat * cols_feat, axis=1)
    dist_sq = norm_rows[:, None] + norm_cols[None, :] - 2.0 * cross_term
    kernel = jnp.exp(-decay_rate * dist_sq)
    weights = grams_tile * kernel
    row_term = grad_scale * (
        jnp.dot(weights, cols_feat, precision=lax.Precision.HIGHEST)
        - jnp.sum(weights, axis=1)[:, None] * rows_feat
    )
    col_term = grad_scale * (
        jnp.dot(weights.T, rows_feat, precision=lax.Precision.HIGHEST)
        - jnp.sum(weights, axis=0)[:, None] * cols_feat
    )
    return (grams_tile, row_term, col_term)


def local(feat_rows, feat_cols, panel_rows, panel_cols, accumulator):
    cols_feat, cols_panel = (
        lax.all_gather(feat_cols, "row", axis=0, tiled=True),
        lax.all_gather(panel_cols, "row", axis=0, tiled=True),
    )
    rows_feat, rows_panel = (
        lax.all_gather(feat_rows, "col", axis=0, tiled=True),
        lax.all_gather(panel_rows, "col", axis=0, tiled=True),
    )
    acc_new, row_term, col_term = local_tile(
        rows_feat, rows_panel, accumulator, cols_feat, cols_panel
    )
    grad_rows = lax.psum_scatter(row_term, "col", scatter_dimension=0, tiled=True)
    grad_cols = lax.psum_scatter(col_term, "row", scatter_dimension=0, tiled=True)
    return (acc_new, grad_rows, grad_cols)


def solution(mesh):
    in_specs = (
        P(("row", "col"), None),
        P(("col", "row"), None),
        P(("row", "col"), None),
        P(("col", "row"), None),
        P("row", "col"),
    )
    out_specs = (P("row", "col"), P(("row", "col"), None), P(("col", "row"), None))
    return jax.shard_map(local, mesh=mesh, in_specs=in_specs, out_specs=out_specs, check_vma=False)
```

profile of v0, /device:TPU:0, one launch (start us, length us, event | category | flops | bytes accessed | tf_op | source)
XLA Modules:
  0.0 166.7 jit_solution(17232750900821269444)
XLA Ops:
  7.2 0.0 copy-start.2
  7.2 0.0 all-gather.8.cloned.1.call-start
  7.2 0.7 all-gather.8.cloned.1.call-update
  7.9 0.0 all-gather.6.cloned.1.call-start
  8.0 0.7 all-gather.6.cloned.1.call-update
  8.7 0.0 all-gather.4.cloned.1.call-start
  8.7 0.7 all-gather.4.cloned.1.call-update
  9.4 0.0 reduce-scatter.5.cloned.1.call-start
  9.4 11.9 %all_gather.15 = f32[256,512]{1,0:T(8,128)S(1)} all-gather(f32[64,512]{1,0:T(8,128)} %param.6), channel_id=1, replica_groups=mesh['row'=4,'col'=8] {'row'}, dimensions={0}, use_global_device_ids=true | all-gather | bytes 655360 | tf_op jit(solution)/shard_map/all_gather | solution.py:31
  21.3 0.1 multiply_reduce_fusion.1
  21.4 13.1 %all-gather.8.cloned.1.call-done = f32[512,512]{1,0:T(8,128)} async-done(((f32[64,512]{1,0:T(8,128)}), f32[512,512]{1,0:T(8,128)}) %all-gather.8.cloned.1.call-update) | async-done | bytes 1048592 | tf_op jit(solution)/shard_map/all_gather | solution.py:35
  34.6 1.4 multiply_reduce_fusion
  36.0 26.6 %all-gather.6.cloned.1.call-done = f32[256,1024]{1,0:T(8,128)} async-done(((f32[64,1024]{1,0:T(8,128)}), f32[256,1024]{1,0:T(8,128)}) %all-gather.6.cloned.1.call-update) | async-done | bytes 1048592 | tf_op jit(solution)/shard_map/all_gather | solution.py:32
  62.6 30.8 %all-gather.4.cloned.1.call-done = f32[512,1024]{1,0:T(8,128)} async-done(((f32[64,1024]{1,0:T(8,128)}), f32[512,1024]{1,0:T(8,128)}) %all-gather.4.cloned.1.call-update) | async-done | bytes 2097168 | tf_op jit(solution)/shard_map/all_gather | solution.py:36
  93.3 3.7 %convolution_add_fusion = f32[512,256]{1,0:T(8,128)S(1)} fusion(f32[512,256]{1,0:T(8,128)S(1)} %copy-done.2, f32[512,1024]{1,0:T(8,128)} %all-gather.4.cloned.1.call-done, f32[256,1024]{1,0:T(8,128)} %all-gather.6.cloned.1.call-done), kind=kOutput, calls=%fused_computation.4 | convolution fusion | flops 1610743808 | bytes 4194304 | tf_op jit(solution)/shard_map/dot_general | solution.py:11
  97.1 0.0 copy-start.1
  97.1 1.2 fusion.6
  98.3 1.9 %fusion.2 = f32[256,512]{1,0:T(8,128)} fusion(f32[512,256]{1,0:T(8,128)S(1)} %get-tuple-element.5, f32[512,512]{1,0:T(8,128)S(1)} %copy-done, f32[256,512]{1,0:T(8,128)S(1)} %all_gather.15, f32[256]{0:T(256)S(1)} %get-tuple-element.3), kind=kOutput, calls=%fused_computation.6 | convolution fusion | flops 805699584 | bytes 2622464 | tf_op jit(solution)/shard_map/dot_general | solution.py:23
  100.2 0.0 reduce-scatter.5.cloned.1.call-update
  100.2 0.0 reduce-scatter.3.cloned.1.call-start
  100.2 2.0 %fusion = f32[512,512]{1,0:T(8,128)} fusion(f32[512,256]{1,0:T(8,128)S(1)} %get-tuple-element.5, f32[256,512]{1,0:T(8,128)S(1)} %all_gather.15, f32[512,512]{1,0:T(8,128)S(1)} %copy-done, f32[512]{0:T(512)S(1)} %get-tuple-element.4), kind=kOutput, calls=%fused_computation.1 | convolution fusion | flops 806092800 | bytes 3147776 | tf_op jit(solution)/shard_map/dot_general | solution.py:19
  102.3 0.0 reduce-scatter.3.cloned.1.call-update
  102.3 22.5 %reduce-scatter.5.cloned.1.call-done = f32[64,512]{1,0:T(8,128)} async-done(((f32[256,512]{1,0:T(8,128)}), f32[64,512]{1,0:T(8,128)}) %reduce-scatter.5.cloned.1.call-update) | async-done | bytes 131088 | tf_op jit(solution)/shard_map/reduce_scatter | solution.py:42
  124.8 35.4 %reduce-scatter.3.cloned.1.call-done = f32[64,512]{1,0:T(8,128)} async-done(((f32[512,512]{1,0:T(8,128)}), f32[64,512]{1,0:T(8,128)}) %reduce-scatter.3.cloned.1.call-update) | async-done | bytes 131088 | tf_op jit(solution)/shard_map/reduce_scatter | solution.py:41
  (4 shorter events, 0.0 us)
Async XLA Ops:
  7.2 86.2 %copy-start.2 = (f32[512,256]{1,0:T(8,128)S(1)}, f32[512,256]{1,0:T(8,128)}, u32[]{:S(2)}) copy-start(f32[512,256]{1,0:T(8,128)} %param.9) | copy-start | bytes 1572868
  7.2 27.4 %all-gather.8.cloned.1.call-start = ((), (), s32[]{:S(2)}) async-start(), calls=%async_computation.4 | async-start | bytes 1179648 | tf_op jit(solution)/shard_map/all_gather | solution.py:35
  7.9 54.6 %all-gather.6.cloned.1.call-start = ((), (), s32[]{:S(2)}) async-start(), calls=%async_computation.3 | async-start | bytes 1310720 | tf_op jit(solution)/shard_map/all_gather | solution.py:32
  8.7 84.7 %all-gather.4.cloned.1.call-start = ((), (), s32[]{:S(2)}) async-start(), calls=%async_computation.2 | async-start | bytes 2359296 | tf_op jit(solution)/shard_map/all_gather | solution.py:36
  9.4 115.4 %reduce-scatter.5.cloned.1.call-start = ((), (), s32[]{:S(2)}) async-start(), calls=%async_computation.6 | async-start | bytes 655360 | tf_op jit(solution)/shard_map/reduce_scatter | solution.py:42
  35.9 61.1 %copy-start = (f32[512,512]{1,0:T(8,128)S(1)}, f32[512,512]{1,0:T(8,128)}, u32[]{:S(2)}) copy-start(f32[512,512]{1,0:T(8,128)} %all-gather.8.cloned.1.call-done) | copy-start | bytes 3145732
  97.1 3.1 %copy-start.1 = (f32[512,256]{1,0:T(8,128)}, f32[512,256]{1,0:T(8,128)S(1)}, u32[]{:S(2)}) copy-start(f32[512,256]{1,0:T(8,128)S(1)} %convolution_add_fusion) | copy-start | bytes 1572868
  100.2 60.0 %reduce-scatter.3.cloned.1.call-start = ((), (), s32[]{:S(2)}) async-start(), calls=%async_computation.5 | async-start | bytes 1179648 | tf_op jit(solution)/shard_map/reduce_scatter | solution.py:41
Sparse Core Ops, SparseCore 0:
  9.6 24.9 all-gather.7
  36.4 26.0 all-gather.5
  64.2 29.1 all-gather.3
  100.3 24.4 reduce-scatter.4
  127.5 32.6 reduce-scatter.2
where the time goes:
time: 167 us
  waiting for transfers between devices  130 us (78%)
  between operations  13.8 us (8%)
  blocking collectives  11.9 us (7%)
  matrix products  8.81 us (5%)
    reduce_scatter x1, waiting for transfers between devices, local(): lax.psum_scatter(row_term, 'col', scatter_dimension=0, tiled=True)  35.4 us
    all_gather x1, waiting for transfers between devices, local(): lax.all_gather(panel_rows, 'col', axis=0, tiled=True)  30.8 us
    all_gather x1, waiting for transfers between devices, local(): lax.all_gather(panel_cols, 'row', axis=0, tiled=True)  26.6 us
    reduce_scatter x1, waiting for transfers between devices, local(): lax.psum_scatter(col_term, 'row', scatter_dimension=0, tiled=True)  22.5 us
    all_gather x1, waiting for transfers between devices, local(): lax.all_gather(feat_rows, 'col', axis=0, tiled=True)  13.1 us
    all_gather x1, blocking collectives, local(): lax.all_gather(feat_cols, 'row', axis=0, tiled=True)  11.9 us
    dot_general x1, matrix products, local_tile(): jnp.dot(rows_panel, cols_panel.T, precision=lax.Precision.HIGHEST)  3.69 us
  transfers between devices with their start and end apart: 5, of which 5 were waited for; matrix products, arithmetic and copies ran while one was open for 2% of the time, Pallas kernels for 0%

commit v1 on v0

v1 whole, which is shorter than its diff:
```python
import functools

import jax
import jax.numpy as jnp
from jax import lax
from jax.experimental import pallas as pl
from jax.experimental.pallas import tpu as pltpu
from jax.sharding import PartitionSpec as P

decay_rate = 0.125
grad_scale = 0.25
MESH = pl.DeviceIdType.MESH
HALVES = 2
LEAD = 2


def split(x):
    hi = x.astype(jnp.bfloat16)
    return hi, (x - hi.astype(jnp.float32)).astype(jnp.bfloat16)


def dot3(a, b, ca, cb):
    dims = (((ca,), (cb,)), ((), ()))
    f = functools.partial(lax.dot_general, dimension_numbers=dims, preferred_element_type=jnp.float32)
    return f(a[0], b[0]) + (f(a[0], b[1]) + f(a[1], b[0]))


def order(n, depth, y, t):
    src, chunk = y * 0, t * 0
    found = y < 0
    for _ in range(depth):
        lead = t < LEAD
        done = jnp.logical_or(lead, t >= LEAD + n * y)
        take = jnp.logical_and(done, jnp.logical_not(found))
        src = jnp.where(take, y, src)
        chunk = jnp.where(take, jnp.where(lead, t, t - n * y), chunk)
        found = jnp.logical_or(found, done)
        y, t = y - 1, t - LEAD
    return src, chunk


def done_slot(n, depth, z, s):
    def seq(y):
        if y == 0:
            return [(0, i) for i in range(n)]
        own = [(y, i) for i in range(n)]
        return own[:LEAD] + seq(y - 1) + own[LEAD:]

    if s == z:
        return -1
    y, ys = (z, s) if s < z else (depth - 1 - z, depth - 1 - s)
    return max(t for t, (a, _) in enumerate(seq(y - 1)) if a == ys)


def plan(n, depth):
    table, need = [], [0] * depth
    for z in range(depth):
        shards = sorted(range(depth), key=lambda s: (done_slot(n, depth, z, s), -abs(s - z)))
        far = [s for s in shards if s != z]
        if z in (0, depth - 1):
            far.insert(len(far) - 1, z)
        else:
            far = sorted(far, key=lambda s: (-abs(s - z), s < z)) + [z]
        table.append(far)
        for j, s in enumerate(far):
            need[j] = max(need[j], done_slot(n, depth, z, s) + 1)
    for j in range(1, depth):
        need[j] = max(need[j], need[j - 1])
    need[0] = max(need[0], n * (depth - 2))
    for j in range(1, depth):
        need[j] = max(need[j], need[0])
    need[-1] = max(need[-1], n * (depth - 1))
    return table, need


def pick(values, at):
    out = jnp.int32(values[0])
    for i, v in enumerate(values[1:], 1):
        out = jnp.where(at == i, jnp.int32(v), out)
    return out


def kernel(R, C, fr, fc, pr, pc, acc, acc_out, gr_out, gc_out,
           rows, cols, chi, clo, ncol, accv, rowp, sibp, chbuf, sumb, colacc, tacc, colr,
           lsem, osem, rrecv, zss, sss, css, crecv, rss, rsr, chs, chrecv, gcs, gcr):
    me_r, me_c = lax.axis_index("row"), lax.axis_index("col")
    z, k = me_c // 2, me_c % 2
    Z = C // 2
    NR, F = fr.shape
    NC = fc.shape[0]
    Q = 1 + pr.shape[1] // F
    n = HALVES * Q
    hr = NR // HALVES
    sibling = (me_r, me_c + 1 - 2 * k)
    place = (z, Z - 1 - z)
    step_to = (2, -2)
    table, need = plan(n, Z)

    def at(start, size, mult):
        return pl.ds(pl.multiple_of(start, mult), size)

    def rchunk(c, i):
        return rows.at[i % Q, at(c * NR + (i // Q) * hr, hr, 8), :]

    def remote(src, dst, ss, rs, dev):
        return pltpu.make_async_remote_copy(src_ref=src, dst_ref=dst, send_sem=ss, recv_sem=rs, device_id=dev, device_id_type=MESH)

    def zcopy(d, zs, i):
        c = 2 * zs + k
        return remote(rchunk(c, i), rchunk(c, i), zss.at[d, zs, i], rrecv.at[c, i], (me_r, me_c + step_to[d]))

    def scopy(zs, core, i):
        c = 2 * zs + core
        return remote(rchunk(c, i), rchunk(c, i), sss.at[zs, i], rrecv.at[c, i], sibling)

    local = []
    for q in range(Q):
        rsrc = fr if q == 0 else pr.at[:, pl.ds((q - 1) * F, F)]
        csrc = fc if q == 0 else pc.at[:, pl.ds((q - 1) * F, F)]
        local.append(pltpu.make_async_copy(rsrc, rows.at[q, at(me_c * NR, NR, 8), :], lsem.at[2 * q]))
        local.append(pltpu.make_async_copy(csrc, cols.at[q, at(me_r * NC, NC, 8), :], lsem.at[2 * q + 1]))
    acc_in = pltpu.make_async_copy(acc, accv, lsem.at[2 * Q])
    for copy in local:
        copy.start()
    acc_in.start()

    barrier = pltpu.get_barrier_semaphore()

    def greet(p, carry):
        pl.semaphore_signal(barrier, inc=1, device_id=((me_r + p) % R, me_c), device_id_type=MESH)
        return carry

    lax.fori_loop(1, R, greet, 0)
    pl.semaphore_signal(barrier, inc=1, device_id=sibling, device_id_type=MESH)
    for d in range(2):
        @pl.when(place[d] < Z - 1)
        def _():
            pl.semaphore_signal(barrier, inc=1, device_id=(me_r, me_c + step_to[d]), device_id_type=MESH)
    for copy in local:
        copy.wait()
    pl.semaphore_wait(barrier, R + (z > 0).astype(jnp.int32) + (z < Z - 1).astype(jnp.int32))

    for d in range(2):
        @pl.when(place[d] < Z - 1)
        def _():
            for i in range(LEAD):
                zcopy(d, z, i).start()

    def col_send(p, q):
        block = cols.at[q, at(me_r * NC, NC, 8), :]
        return remote(block, block, css.at[p, q], crecv.at[me_r, q], ((me_r + p) % R, me_c))

    def col_recv(p, q):
        src = (me_r + p) % R
        block = cols.at[q, at(src * NC, NC, 8), :]
        return remote(block, block, css.at[p, q], crecv.at[src, q], ((me_r + p) % R, me_c))

    def push_cols(p, carry):
        for q in range(Q):
            col_send(p, q).start()
        return carry

    lax.fori_loop(1, R, push_cols, 0)
    for d in range(2):
        @pl.when(place[d] == 0)
        def _():
            for i in range(LEAD, n):
                zcopy(d, z, i).start()
    for i in range(n):
        scopy(z, k, i).start()

    def slot(t, carry):
        for d in range(2):
            y = place[d]

            @pl.when(t < n * y)
            def _():
                ys, i = order(n, Z, y - 1, t)
                zs = ys if d == 0 else Z - 1 - ys
                zcopy(d, zs, i).wait_recv()

                @pl.when(y < Z - 1)
                def _():
                    zcopy(d, zs, i).start()

                scopy(zs, k, i).start()

                @pl.when(jnp.logical_and(t == n * y - 1, y < Z - 1))
                def _():
                    for j in range(LEAD, n):
                        zcopy(d, z, j).start()

        return carry

    lax.fori_loop(0, need[0], slot, 0)

    def await_cols(p, carry):
        for q in range(Q):
            col_recv(p, q).wait_recv()
        return carry

    lax.fori_loop(1, R, await_cols, 0)
    acc_in.wait()
    for q in range(Q):
        hi, lo = split(cols[q])
        chi[q] = hi
        clo[q] = lo
    feats = cols[0]
    ncol[...] = lax.dot_general(
        jnp.ones((8, F), jnp.float32), feats * feats, (((1,), (1,)), ((), ())),
        precision=lax.Precision.HIGHEST, preferred_element_type=jnp.float32)
    colacc[...] = jnp.zeros_like(colacc)
    tacc[...] = jnp.zeros_like(tacc)

    def shard_of(j):
        out = pick([table[0][i] for i in range(Z)], j)
        for place_z in range(1, Z):
            out = jnp.where(z == place_z, pick([table[place_z][i] for i in range(Z)], j), out)
        return out

    def exchange(zs):
        return remote(rowp.at[at(zs * 2 * NR + (1 - k) * NR, NR, 8), :], sibp.at[zs], rss.at[zs], rsr.at[zs], sibling)

    def out_copy(zs):
        block = at(zs * 2 * NR, 2 * NR, 8)
        return pltpu.make_async_copy(accv.at[block, :], acc_out.at[block, :], osem.at[zs])

    def compute(zs):
        for i in range(n):
            scopy(zs, 1 - k, i).wait_recv()
        block = at(zs * 2 * NR, 2 * NR, 8)
        f = rows[0, block, :]
        cross = lax.dot_general(f, cols[0], (((1,), (1,)), ((), ())), precision=lax.Precision.HIGHEST, preferred_element_type=jnp.float32)
        g = accv[block, :]
        for q in range(1, Q):
            g = g + dot3(split(rows[q, block, :]), (chi[q], clo[q]), 1, 1)
        accv[block, :] = g
        out_copy(zs).start()
        dist = jnp.sum(f * f, axis=1, keepdims=True) + ncol[0:1, :] - 2.0 * cross
        w = g * jnp.exp(-decay_rate * dist)
        s = jnp.sum(w, axis=1, keepdims=True)
        rowp[block, :] = grad_scale * (dot3(split(w), (chi[0], clo[0]), 1, 0) - s * f)
        exchange(zs).start()
        colacc[...] += dot3(split(w.T), split(f), 1, 0)
        tacc[...] += jnp.broadcast_to(jnp.sum(w, axis=0, keepdims=True), tacc.shape)

    def chain_copy(d, zs):
        return remote(sumb.at[zs], chbuf.at[d, zs], chs.at[zs], chrecv.at[d, zs], (me_r, me_c + step_to[d]))

    def chain(zs):
        exchange(zs).wait_recv()
        sumb[zs] = rowp[at(zs * 2 * NR + k * NR, NR, 8), :] + sibp[zs]
        for d in range(2):
            @pl.when(zs > z if d == 0 else zs < z)
            def _():
                @pl.when(place[d] > 0)
                def _():
                    chain_copy(d, zs).wait_recv()
                    sumb[zs] += chbuf[d, zs]

                chain_copy(d, zs).start()

    needs = need + [need[-1]]

    def step(j, carry):
        @pl.when(j > 0)
        def _():
            lax.fori_loop(pick(needs, j - 1), pick(needs, j), slot, 0)

        compute(shard_of(j))

        @pl.when(jnp.logical_and(j > 0, j < Z - 1))
        def _():
            chain(shard_of(j - 1))

        return carry

    lax.fori_loop(0, Z, step, 0)

    def grad_send(p):
        to = (me_r + p) % R
        return remote(colacc.at[at(to * NC, NC, 8), :], colr.at[me_r], gcs.at[p], gcr.at[me_r], (to, me_c))

    def grad_recv(p):
        src = (me_r + p) % R
        return remote(colacc.at[at(src * NC, NC, 8), :], colr.at[src], gcs.at[p], gcr.at[src], (src, me_c))

    tcol = jnp.broadcast_to(tacc[0:1, :], (128, tacc.shape[1])).T[:, 0:1]
    colacc[...] = grad_scale * (colacc[...] - tcol * cols[0])

    def push_grad(p, carry):
        grad_send(p).start()
        return carry

    lax.fori_loop(1, R, push_grad, 0)

    def last_chain(j, carry):
        chain(shard_of(j))
        return carry

    lax.fori_loop(max(Z - 2, 0), Z, last_chain, 0)
    for d in range(2):
        @pl.when(place[d] > 0)
        def _():
            chain_copy(d, z).wait_recv()
            sumb[z] += chbuf[d, z]
    gr_out[...] = sumb[z]

    gc_out[...] = colacc[at(me_r * NC, NC, 8), :]

    def add_grad(p, carry):
        grad_recv(p).wait_recv()
        gc_out[...] += colr[(me_r + p) % R]
        return carry

    lax.fori_loop(1, R, add_grad, 0)

    def drain_peer(p, carry):
        for q in range(Q):
            col_send(p, q).wait_send()
        grad_send(p).wait_send()
        return carry

    lax.fori_loop(1, R, drain_peer, 0)
    for d in range(2):
        y = place[d]

        @pl.when(y < Z - 1)
        def _():
            def drain(ys, carry):
                zs = ys if d == 0 else Z - 1 - ys
                for i in range(n):
                    zcopy(d, zs, i).wait_send()
                return carry

            lax.fori_loop(0, y + 1, drain, 0)

    def drain_shard(zs, carry):
        for i in range(n):
            scopy(zs, k, i).wait_send()
        exchange(zs).wait_send()
        out_copy(zs).wait()

        for d in range(2):
            @pl.when(zs > z if d == 0 else zs < z)
            def _():
                chain_copy(d, zs).wait_send()
        return carry

    lax.fori_loop(0, Z, drain_shard, 0)


def solution(mesh):
    R, C = mesh.shape["row"], mesh.shape["col"]
    in_specs = (
        P(("row", "col"), None),
        P(("col", "row"), None),
        P(("row", "col"), None),
        P(("col", "row"), None),
        P("row", "col"),
    )
    out_specs = (P("row", "col"), P(("row", "col"), None), P(("col", "row"), None))

    def local(fr, fc, pr, pc, acc):
        NR, F = fr.shape
        NC = fc.shape[0]
        Q = 1 + pr.shape[1] // F
        Z, n = C // 2, HALVES * Q
        f32, bf16 = jnp.float32, jnp.bfloat16
        V, D = pltpu.VMEM, pltpu.SemaphoreType.DMA
        hbm = pl.BlockSpec(memory_space=pl.ANY)
        vmem = pl.BlockSpec(memory_space=pltpu.VMEM)
        return pl.pallas_call(
            functools.partial(kernel, R, C),
            out_shape=(
                jax.ShapeDtypeStruct(acc.shape, f32),
                jax.ShapeDtypeStruct(fr.shape, f32),
                jax.ShapeDtypeStruct(fc.shape, f32),
            ),
            in_specs=[hbm] * 5,
            out_specs=(hbm, vmem, vmem),
            scratch_shapes=[
                V((Q, C * NR, F), f32), V((Q, R * NC, F), f32),
                V((Q, R * NC, F), bf16), V((Q, R * NC, F), bf16),
                V((8, R * NC), f32), V(acc.shape, f32),
                V((C * NR, F), f32), V((Z, NR, F), f32), V((2, Z, NR, F), f32), V((Z, NR, F), f32),
                V((R * NC, F), f32), V((8, R * NC), f32), V((R, NC, F), f32),
                D((2 * Q + 1,)), D((Z,)), D((C, n)), D((2, Z, n)), D((Z, n)),
                D((R, Q)), D((R, Q)), D((Z,)), D((Z,)), D((Z,)), D((2, Z)), D((R,)), D((R,)),
            ],
            compiler_params=pltpu.CompilerParams(
                collective_id=0, has_side_effects=True, vmem_limit_bytes=56 * 1024 * 1024),
        )(fr, fc, pr, pc, acc)

    return jax.shard_map(local, mesh=mesh, in_specs=in_specs, out_specs=out_specs, check_vma=False)
```

time: 167 us -> 56.4 us (0.34)
  the two profiles are of different devices: /device:TPU:0 before, /device:TPU:17 now
where the time goes in v1:
time: 56.4 us; the launch traced here: 56.2 us
  Pallas kernels  52.1 us (92%)
  local copies, waits for them, and re-layouts  3.51 us (6%)
  between operations  0.65 us (1%)
    pallas_call x1, Pallas kernels, local(): pl.pallas_call(functools.partial(kernel, R, C), out_shape=(jax.ShapeDtype...  52.1 us
    unnamed x7, local copies, waits for them, and re-layouts  3.51 us

profile of v1, /device:TPU:17, one launch (start us, length us, event | category | flops | bytes accessed | tf_op | source)
XLA Modules:
  0.0 56.2 jit_solution(9622926372781757318)
XLA Ops:
  0.6 52.1 %shard_map.76 = (f32[512,256]{1,0:T(8,128)}, f32[64,512]{1,0:T(8,128)}, f32[64,512]{1,0:T(8,128)}) custom-call(f32[64,512]{1,0:T(8,128)} %fr.1, f32[64,512]{1,0:T(8,128)} %fc.1, f32[64,1024]{1,0:T(8,128)} %pr.1, f32[64,1024]{1,0:T(8,128)} %pc.1, f32[512,256]{1,0:T(8,128)} %acc.1), custom_call_target="tpu_custom_call" | custom-call | tf_op jit(solution)/shard_map/pallas_call | solution.py:373
  52.7 0.0 copy-start.1
  52.7 1.9 %copy.11 = f32[512,256]{1,0:T(8,128)} copy(f32[512,256]{1,0:T(8,128)} %get-tuple-element.6) | data formatting | bytes 1048576
  54.6 0.0 copy-done.1
  54.6 0.0 copy-start
  54.6 0.7 %copy.12 = f32[64,512]{1,0:T(8,128)} copy(f32[64,512]{1,0:T(8,128)S(1)} %copy-done.1) | data formatting | bytes 262144
  55.3 0.3 copy-done
  55.6 0.7 %copy.13 = f32[64,512]{1,0:T(8,128)} copy(f32[64,512]{1,0:T(8,128)S(1)} %copy-done) | data formatting | bytes 262144
Async XLA Ops:
  52.7 1.9 %copy-start.1 = (f32[64,512]{1,0:T(8,128)S(1)}, f32[64,512]{1,0:T(8,128)}, u32[]{:S(2)}) copy-start(f32[64,512]{1,0:T(8,128)} %get-tuple-element.7) | copy-start | bytes 393220
  54.6 1.0 %copy-start = (f32[64,512]{1,0:T(8,128)S(1)}, f32[64,512]{1,0:T(8,128)}, u32[]{:S(2)}) copy-start(f32[64,512]{1,0:T(8,128)} %get-tuple-element.8) | copy-start | bytes 393220

commit v2 on v1

--- a/solution.py
+++ b/solution.py
@@ -11,7 +11,7 @@
 grad_scale = 0.25
 MESH = pl.DeviceIdType.MESH
 HALVES = 2
-LEAD = 2
+LEAD = 3
 
 
 def split(x):
@@ -80,9 +80,9 @@
     return out
 
 
-def kernel(R, C, fr, fc, pr, pc, acc, acc_out, gr_out, gc_out,
-           rows, cols, chi, clo, ncol, accv, rowp, sibp, chbuf, sumb, colacc, tacc, colr,
-           lsem, osem, rrecv, zss, sss, css, crecv, rss, rsr, chs, chrecv, gcs, gcr):
+def kernel(R, C, fr, fc, pr, pc, acc, accv, gr_out, gc_out,
+           rows, cols, chi, clo, ncol, rowp, sibp, chbuf, sumb, colacc, tacc, colr,
+           lsem, rrecv, zss, sss, css, crecv, rss, rsr, chs, chrecv, gcs, gcr):
     me_r, me_c = lax.axis_index("row"), lax.axis_index("col")
     z, k = me_c // 2, me_c % 2
     Z = C // 2
@@ -221,10 +221,6 @@
     def exchange(zs):
         return remote(rowp.at[at(zs * 2 * NR + (1 - k) * NR, NR, 8), :], sibp.at[zs], rss.at[zs], rsr.at[zs], sibling)
 
-    def out_copy(zs):
-        block = at(zs * 2 * NR, 2 * NR, 8)
-        return pltpu.make_async_copy(accv.at[block, :], acc_out.at[block, :], osem.at[zs])
-
     def compute(zs):
         for i in range(n):
             scopy(zs, 1 - k, i).wait_recv()
@@ -235,7 +231,6 @@
         for q in range(1, Q):
             g = g + dot3(split(rows[q, block, :]), (chi[q], clo[q]), 1, 1)
         accv[block, :] = g
-        out_copy(zs).start()
         dist = jnp.sum(f * f, axis=1, keepdims=True) + ncol[0:1, :] - 2.0 * cross
         w = g * jnp.exp(-decay_rate * dist)
         s = jnp.sum(w, axis=1, keepdims=True)
@@ -339,7 +334,6 @@
         for i in range(n):
             scopy(zs, k, i).wait_send()
         exchange(zs).wait_send()
-        out_copy(zs).wait()
 
         for d in range(2):
             @pl.when(zs > z if d == 0 else zs < z)
@@ -370,26 +364,24 @@
         V, D = pltpu.VMEM, pltpu.SemaphoreType.DMA
         hbm = pl.BlockSpec(memory_space=pl.ANY)
         vmem = pl.BlockSpec(memory_space=pltpu.VMEM)
-        return pl.pallas_call(
+        shapes = (acc.shape, fr.shape, fc.shape)
+        made = pl.pallas_call(
             functools.partial(kernel, R, C),
-            out_shape=(
-                jax.ShapeDtypeStruct(acc.shape, f32),
-                jax.ShapeDtypeStruct(fr.shape, f32),
-                jax.ShapeDtypeStruct(fc.shape, f32),
-            ),
+            out_shape=tuple(pltpu.VMEM(s, f32) for s in shapes),
             in_specs=[hbm] * 5,
-            out_specs=(hbm, vmem, vmem),
+            out_specs=(vmem,) * 3,
             scratch_shapes=[
                 V((Q, C * NR, F), f32), V((Q, R * NC, F), f32),
                 V((Q, R * NC, F), bf16), V((Q, R * NC, F), bf16),
-                V((8, R * NC), f32), V(acc.shape, f32),
+                V((8, R * NC), f32),
                 V((C * NR, F), f32), V((Z, NR, F), f32), V((2, Z, NR, F), f32), V((Z, NR, F), f32),
                 V((R * NC, F), f32), V((8, R * NC), f32), V((R, NC, F), f32),
-                D((2 * Q + 1,)), D((Z,)), D((C, n)), D((2, Z, n)), D((Z, n)),
+                D((2 * Q + 1,)), D((C, n)), D((2, Z, n)), D((Z, n)),
                 D((R, Q)), D((R, Q)), D((Z,)), D((Z,)), D((Z,)), D((2, Z)), D((R,)), D((R,)),
             ],
             compiler_params=pltpu.CompilerParams(
                 collective_id=0, has_side_effects=True, vmem_limit_bytes=56 * 1024 * 1024),
         )(fr, fc, pr, pc, acc)
+        return tuple(made)
 
     return jax.shard_map(local, mesh=mesh, in_specs=in_specs, out_specs=out_specs, check_vma=False)

time: 56.4 us -> 52.1 us (0.924)
  Pallas kernels: 52.1 us -> 49.2 us
  local copies, waits for them, and re-layouts: 3.51 us -> 2.11 us
    pallas_call x1, Pallas kernels: 52.1 us -> 49.2 us  [local(): pl.pallas_call(functools.partial(kernel, R, C), out_shape=tuple((pltpu.VM...]
    unnamed x7 -> x3, local copies, waits for them, and re-layouts: 3.51 us -> 2.11 us
where the time goes in v2:
time: 52.1 us; the launch traced here: 51.9 us
  Pallas kernels  49.2 us (94%)
  local copies, waits for them, and re-layouts  2.11 us (4%)
  between operations  0.64 us (1%)
    pallas_call x1, Pallas kernels, local(): pl.pallas_call(functools.partial(kernel, R, C), out_shape=tuple((pltpu.VM...  49.2 us
    unnamed x3, local copies, waits for them, and re-layouts  2.11 us

profile of v2, /device:TPU:17, one launch (start us, length us, event | category | flops | bytes accessed | tf_op | source)
XLA Modules:
  0.0 51.9 jit_solution(12980777009384765295)
XLA Ops:
  0.6 49.2 %shard_map.76 = (f32[512,256]{1,0:T(8,128)S(1)}, f32[64,512]{1,0:T(8,128)S(1)}, f32[64,512]{1,0:T(8,128)S(1)}) custom-call(f32[64,512]{1,0:T(8,128)} %fr.1, f32[64,512]{1,0:T(8,128)} %fc.1, f32[64,1024]{1,0:T(8,128)} %pr.1, f32[64,1024]{1,0:T(8,128)} %pc.1, f32[512,256]{1,0:T(8,128)} %acc.1), custom_call_target="tpu_custom_call" | custom-call | tf_op jit(solution)/shard_map/pallas_call | solution.py:368
  49.8 0.8 %copy.11 = f32[512,256]{1,0:T(8,128)} copy(f32[512,256]{1,0:T(8,128)S(1)} %get-tuple-element.3) | data formatting | bytes 1048576
  50.6 0.7 %copy.12 = f32[64,512]{1,0:T(8,128)} copy(f32[64,512]{1,0:T(8,128)S(1)} %get-tuple-element.4) | data formatting | bytes 262144
  51.3 0.7 %copy.13 = f32[64,512]{1,0:T(8,128)} copy(f32[64,512]{1,0:T(8,128)S(1)} %get-tuple-element.5) | data formatting | bytes 262144

commit v3 on v2

--- a/solution.py
+++ b/solution.py
@@ -12,6 +12,7 @@
 MESH = pl.DeviceIdType.MESH
 HALVES = 2
 LEAD = 3
+RELAY_SLOTS = 2
 
 
 def split(x):
@@ -60,7 +61,7 @@
         if z in (0, depth - 1):
             far.insert(len(far) - 1, z)
         else:
-            far = sorted(far, key=lambda s: (-abs(s - z), s < z)) + [z]
+            far = sorted(far, key=lambda s: 2 * z + depth - 1 - s if s > z else 2 * (depth - 1 - z) + s) + [z]
         table.append(far)
         for j, s in enumerate(far):
             need[j] = max(need[j], done_slot(n, depth, z, s) + 1)
@@ -82,7 +83,7 @@
 
 def kernel(R, C, fr, fc, pr, pc, acc, accv, gr_out, gc_out,
            rows, cols, chi, clo, ncol, rowp, sibp, chbuf, sumb, colacc, tacc, colr,
-           lsem, rrecv, zss, sss, css, crecv, rss, rsr, chs, chrecv, gcs, gcr):
+           lsem, rrecv, zss, sss, css, crecv, rss, rsr, chs, chrecv, gcs, gcr, ys, yr):
     me_r, me_c = lax.axis_index("row"), lax.axis_index("col")
     z, k = me_c // 2, me_c % 2
     Z = C // 2
@@ -160,7 +161,28 @@
             col_send(p, q).start()
         return carry
 
-    lax.fori_loop(1, R, push_cols, 0)
+    square = R == 4
+    near = (me_r // 2 * 2 + 1 - me_r % 2, (1 - me_r // 2) * 2 + me_r % 2)
+    across = R - 1 - me_r
+
+    def own_push(axis, q):
+        block = cols.at[q, at(me_r * NC, NC, 8), :]
+        return remote(block, block, css.at[axis, q], crecv.at[me_r, q], (near[axis], me_c))
+
+    def own_arrive(axis, q):
+        block = cols.at[q, at(near[axis] * NC, NC, 8), :]
+        return remote(block, block, css.at[axis, q], crecv.at[near[axis], q], (near[axis], me_c))
+
+    def relay(axis, q, owner):
+        block = cols.at[q, at(owner * NC + axis * (NC // 2), NC // 2, 8), :]
+        return remote(block, block, ys.at[axis, q], yr.at[axis, q], (near[1 - axis], me_c))
+
+    if square:
+        for q in range(Q):
+            for axis in range(2):
+                own_push(axis, q).start()
+    else:
+        lax.fori_loop(1, R, push_cols, 0)
     for d in range(2):
         @pl.when(place[d] == 0)
         def _():
@@ -192,14 +214,28 @@
 
         return carry
 
-    lax.fori_loop(0, need[0], slot, 0)
+    passed = 0
+    if square:
+        for q in range(Q):
+            upto = min(RELAY_SLOTS * (q + 1), need[0])
+            lax.fori_loop(passed, upto, slot, 0)
+            passed = upto
+            for axis in range(2):
+                own_arrive(axis, q).wait_recv()
+                relay(axis, q, near[axis]).start()
+    lax.fori_loop(passed, need[0], slot, 0)
 
     def await_cols(p, carry):
         for q in range(Q):
             col_recv(p, q).wait_recv()
         return carry
 
-    lax.fori_loop(1, R, await_cols, 0)
+    if square:
+        for q in range(Q):
+            for axis in range(2):
+                relay(axis, q, across).wait_recv()
+    else:
+        lax.fori_loop(1, R, await_cols, 0)
     acc_in.wait()
     for q in range(Q):
         hi, lo = split(cols[q])
@@ -256,6 +292,7 @@
                 chain_copy(d, zs).start()
 
     needs = need + [need[-1]]
+    at_end = jnp.logical_or(z == 0, z == Z - 1)
 
     def step(j, carry):
         @pl.when(j > 0)
@@ -264,9 +301,9 @@
 
         compute(shard_of(j))
 
-        @pl.when(jnp.logical_and(j > 0, j < Z - 1))
-        def _():
-            chain(shard_of(j - 1))
+        @pl.when(jnp.logical_and(at_end, j < Z - 2))
+        def _():
+            chain(shard_of(j))
 
         return carry
 
@@ -293,7 +330,7 @@
         chain(shard_of(j))
         return carry
 
-    lax.fori_loop(max(Z - 2, 0), Z, last_chain, 0)
+    lax.fori_loop(jnp.where(at_end, max(Z - 2, 0), 0), Z, last_chain, 0)
     for d in range(2):
         @pl.when(place[d] > 0)
         def _():
@@ -311,12 +348,18 @@
     lax.fori_loop(1, R, add_grad, 0)
 
     def drain_peer(p, carry):
-        for q in range(Q):
-            col_send(p, q).wait_send()
+        if not square:
+            for q in range(Q):
+                col_send(p, q).wait_send()
         grad_send(p).wait_send()
         return carry
 
     lax.fori_loop(1, R, drain_peer, 0)
+    if square:
+        for q in range(Q):
+            for axis in range(2):
+                own_push(axis, q).wait_send()
+                relay(axis, q, near[axis]).wait_send()
     for d in range(2):
         y = place[d]
 
@@ -377,7 +420,7 @@
                 V((C * NR, F), f32), V((Z, NR, F), f32), V((2, Z, NR, F), f32), V((Z, NR, F), f32),
                 V((R * NC, F), f32), V((8, R * NC), f32), V((R, NC, F), f32),
                 D((2 * Q + 1,)), D((C, n)), D((2, Z, n)), D((Z, n)),
-                D((R, Q)), D((R, Q)), D((Z,)), D((Z,)), D((Z,)), D((2, Z)), D((R,)), D((R,)),
+                D((R, Q)), D((R, Q)), D((Z,)), D((Z,)), D((Z,)), D((2, Z)), D((R,)), D((R,)), D((2, Q)), D((2, Q)),
             ],
             compiler_params=pltpu.CompilerParams(
                 collective_id=0, has_side_effects=True, vmem_limit_bytes=56 * 1024 * 1024),

time: 52.1 us -> 48.9 us (0.939)
  the two profiles are of different devices: /device:TPU:17 before, /device:TPU:0 now
where the time goes in v3:
time: 48.9 us; the launch traced here: 48.7 us
  Pallas kernels  46 us (94%)
  local copies, waits for them, and re-layouts  2.11 us (4%)
  between operations  0.64 us (1%)
    pallas_call x1, Pallas kernels, local(): pl.pallas_call(functools.partial(kernel, R, C), out_shape=tuple((pltpu.VM...  46 us
    unnamed x3, local copies, waits for them, and re-layouts  2.11 us

profile of v3, /device:TPU:0, one launch (start us, length us, event | category | flops | bytes accessed | tf_op | source)
XLA Modules:
  0.0 48.7 jit_solution(2312249296472130126)
XLA Ops:
  0.6 46.0 %shard_map.76 = (f32[512,256]{1,0:T(8,128)S(1)}, f32[64,512]{1,0:T(8,128)S(1)}, f32[64,512]{1,0:T(8,128)S(1)}) custom-call(f32[64,512]{1,0:T(8,128)} %fr.1, f32[64,512]{1,0:T(8,128)} %fc.1, f32[64,1024]{1,0:T(8,128)} %pr.1, f32[64,1024]{1,0:T(8,128)} %pc.1, f32[512,256]{1,0:T(8,128)} %acc.1), custom_call_target="tpu_custom_call" | custom-call | tf_op jit(solution)/shard_map/pallas_call | solution.py:411
  46.6 0.8 %copy.11 = f32[512,256]{1,0:T(8,128)} copy(f32[512,256]{1,0:T(8,128)S(1)} %get-tuple-element.3) | data formatting | bytes 1048576
  47.4 0.7 %copy.12 = f32[64,512]{1,0:T(8,128)} copy(f32[64,512]{1,0:T(8,128)S(1)} %get-tuple-element.4) | data formatting | bytes 262144
  48.1 0.7 %copy.13 = f32[64,512]{1,0:T(8,128)} copy(f32[64,512]{1,0:T(8,128)S(1)} %get-tuple-element.5) | data formatting | bytes 262144
